TPU v7x, 256 devices: a whole 4x4x8 slice. The times are simulated.
256 devices in a mesh: expert: 4 (over z_lo), dp: 64 (over y, x, z_hi, core).
Axes of the slice: x: 4, y: 4, z: 8 (z_hi: 2, z_lo: 4; z = z_hi * 4 + z_lo), core: 2. Of those that a mesh axis runs over, the one named last changes fastest.
Arguments:
- act_attn: bfloat16 [65536, 256], P(('expert', 'dp')), may hold values from -10 to 10
- dy_attn: bfloat16 [65536, 6144], P(('expert', 'dp')), may hold values from -10 to 10
- act_exp: bfloat16 [4, 8192, 128], P('expert', 'dp'), may hold values from -10 to 10
- dy_exp: bfloat16 [4, 8192, 6144], P('expert', 'dp'), may hold values from -10 to 10
- w_attn: float32 [256, 6144], P(('expert', 'dp')), may hold values from -0.3 to 0.3
- m_attn: float32 [256, 6144], P(('expert', 'dp')), may hold values from -1.5 to 1.5
- v_attn: float32 [256, 6144], P(('expert', 'dp')), may hold values from 0.05 to 1
- w_exp: float32 [4, 128, 6144], P('expert', 'dp'), may hold values from -0.3 to 0.3
- m_exp: float32 [4, 128, 6144], P('expert', 'dp'), may hold values from -1.5 to 1.5
- v_exp: float32 [4, 128, 6144], P('expert', 'dp'), may hold values from 0.05 to 1
Outputs:
- w_attn_new: float32 [256, 6144], P(('expert', 'dp'))
- m_attn_new: float32 [256, 6144], P(('expert', 'dp'))
- v_attn_new: float32 [256, 6144], P(('expert', 'dp'))
- w_exp_new: float32 [4, 128, 6144], P('expert', 'dp')
- m_exp_new: float32 [4, 128, 6144], P('expert', 'dp')
- v_exp_new: float32 [4, 128, 6144], P('expert', 'dp')
- attn_weights: bfloat16 [256, 6144], replicated
- expert_weights: bfloat16 [4, 128, 6144], P('expert')
All inputs are finite; a program needn't handle non-finite values.
Results may differ from a plain program's by a relative error of at most 0.0075.
Values may be sent and summed in bfloat16 or wider, within the bound.
A program may use at most 64 MiB of HBM per device.

v0:
```python
import math
import jax
import jax.numpy as jnp
from jax import lax
from jax.sharding import PartitionSpec as P

beta_first = 0.9
beta_second = 0.95
bias_first = 1.0 - 0.9**10
bias_second = 1.0 - 0.95**10
learn_rate = 0.01
decay_rate = 0.1
adam_eps = 1e-08


def contract_rows(left, right):
    return lax.dot_general(
        left, right, (((0,), (0,)), ((), ())), preferred_element_type=jnp.float32
    )


def adamw(grad, weight, moment, second, factor):
    scaled = factor * grad
    moment_new = beta_first * moment + (1.0 - beta_first) * scaled
    second_new = beta_second * second + (1.0 - beta_second) * scaled * scaled
    update = moment_new / bias_first / (jnp.sqrt(second_new / bias_second) + adam_eps)
    weight_new = weight - learn_rate * (update + decay_rate * weight)
    return (weight_new, moment_new, second_new)


def body(act_attn, dy_attn, act_exp, dy_exp, w_attn, m_attn, v_attn, w_exp, m_exp, v_exp):
    width = w_attn.shape[1]
    n_expert = lax.axis_size("expert")
    total_params = width * (act_attn.shape[1] + n_expert * act_exp.shape[2])
    limit = 0.5 * math.sqrt(total_params)
    g_attn = lax.psum_scatter(
        contract_rows(act_attn, dy_attn), ("expert", "dp"), scatter_dimension=0, tiled=True
    )
    sq_attn = jnp.sum(g_attn * g_attn)
    local_act = act_exp[0]
    local_dy = dy_exp[0]
    g_exp = lax.psum_scatter(
        contract_rows(local_act, local_dy), "dp", scatter_dimension=0, tiled=True
    )
    sq_exp = jnp.sum(g_exp * g_exp)
    summed = lax.psum((sq_attn, sq_exp), ("expert", "dp"))
    total = summed[0] + summed[1]
    norm = jnp.sqrt(total)
    factor = jnp.minimum(1.0, limit / (norm + 1e-06))
    wa_new, ma_new, va_new = adamw(g_attn, w_attn, m_attn, v_attn, factor)
    we_new, me_new, ve_new = adamw(g_exp[None], w_exp, m_exp, v_exp, factor)
    attn_half = wa_new.astype(jnp.bfloat16)
    attn_full = lax.all_gather(attn_half, ("expert", "dp"), axis=0, tiled=True)
    expert_full = lax.all_gather(we_new.astype(jnp.bfloat16), "dp", axis=1, tiled=True)
    return (wa_new, ma_new, va_new, we_new, me_new, ve_new, attn_full, expert_full)


def solution(mesh):
    return jax.shard_map(
        body,
        mesh=mesh,
        in_specs=(
            P(("expert", "dp"), None),
            P(("expert", "dp"), None),
            P("expert", "dp", None),
            P("expert", "dp", None),
            P(("expert", "dp"), None),
            P(("expert", "dp"), None),
            P(("expert", "dp"), None),
            P("expert", "dp", None),
            P("expert", "dp", None),
            P("expert", "dp", None),
        ),
        out_specs=(
            P(("expert", "dp"), None),
            P(("expert", "dp"), None),
            P(("expert", "dp"), None),
            P("expert", "dp", None),
            P("expert", "dp", None),
            P("expert", "dp", None),
            P(),
            P("expert", None, None),
        ),
        check_vma=False,
    )
```

profile of v0, /device:TPU:32, one launch (start us, length us, event | category | flops | bytes accessed | tf_op | source)
XLA Modules:
  0.0 1681.9 jit_solution(16280890841784815197)
XLA Ops:
  7.2 0.0 copy-start
  7.2 0.0 all-reduce.5.cloned.1.call-start
  7.2 1.8 copy-done
  9.1 4.5 fusion.9
  13.6 0.0 copy-start.4
  13.6 0.0 all-reduce.5.cloned.1.call-update
  13.6 0.0 copy-start.8
  13.6 0.0 copy-start.1
  13.7 0.0 copy-start.2
  13.7 0.0 copy-start.3
  13.7 0.0 copy-start.5
  13.7 0.0 copy-start.6
  13.7 0.0 copy-start.7
  13.7 0.0 all-reduce.7.cloned.1.call-start
  13.8 0.6 copy-done.4
  14.4 3.7 fusion
  18.0 0.0 all-reduce.7.cloned.1.call-update
  18.1 0.0 all-gather.4.cloned.1.call-start
  18.1 0.0 copy-done.8
  18.1 0.6 dynamic-slice.1
  19.4 268.9 %all-reduce.5.cloned.1.call-done = f32[256,6144]{1,0:T(8,128)} async-done(((f32[256,6144]{1,0:T(8,128)}), f32[256,6144]{1,0:T(8,128)}) %all-reduce.5.cloned.1.call-update) | async-done | bytes 6291472
  288.3 1.6 multiply_reduce_fusion.1
  289.9 795.2 %all-reduce.7.cloned.1.call-done = f32[128,6144]{1,0:T(8,128)} async-done(((f32[128,6144]{1,0:T(8,128)}), f32[128,6144]{1,0:T(8,128)}) %all-reduce.7.cloned.1.call-update) | async-done | bytes 3145744
  1085.1 1.6 multiply_reduce_fusion
  1088.0 78.6 %psum.16 = f32[]{:T(128)} all-reduce(f32[]{:T(128)S(6)} %add.44), channel_id=1, replica_groups=mesh['expert'=4,'dp'=64] {'expert','dp'}, use_global_device_ids=true, to_apply=%region_2.0 | all-reduce | flops 1 | bytes 8 | tf_op jit(solution)/shard_map/psum | solution.py:46
  1167.4 0.0 copy-done.1
  1167.4 0.0 copy-done.2
  1167.4 0.0 copy-done.3
  1167.4 1.8 fusion.6
  1169.2 0.7 copy.20
  1169.8 0.0 all-gather.4.cloned.1.call-update
  1169.9 0.0 all-gather.6.cloned.1.call-start
  1169.9 0.0 copy-done.5
  1169.9 0.0 copy-done.6
  1169.9 0.0 copy-done.7
  1169.9 1.8 convert_bitcast_fusion
  1171.7 0.0 all-gather.6.cloned.1.call-update
  1171.7 81.3 %all-gather.4.cloned.1.call-done = bf16[1,128,6144]{2,0,1:T(2,128)(2,1)} async-done(((bf16[1,2,6144]{2,0,1:T(2,128)(2,1)}), bf16[1,128,6144]{2,0,1:T(2,128)(2,1)}) %all-gather.4.cloned.1.call-update) | async-done | bytes 1572880 | tf_op jit(solution)/shard_map/all_gather | solution.py:54
  1253.0 3.9 copy.21
  1256.9 412.2 %all-gather.6.cloned.1.call-done = bf16[256,1,6144]{2,1,0:T(2,128)(2,1)} async-done(((bf16[1,1,6144]{2,1,0:T(2,128)(2,1)}), bf16[256,1,6144]{2,1,0:T(2,128)(2,1)}) %all-gather.6.cloned.1.call-update) | async-done | bytes 3145744 | tf_op jit(solution)/shard_map/all_gather | solution.py:53
  1669.1 6.2 copy.24
Async XLA Ops:
  7.2 1.9 copy-start
  7.2 281.1 %all-reduce.5.cloned.1.call-start = ((), (), s32[]{:S(2)}) async-start(), calls=%async_computation.2 | async-start | bytes 12582912
  13.6 0.8 copy-start.4
  13.6 4.5 copy-start.8
  13.6 1153.7 %copy-start.1 = (f32[1,2,6144]{2,1,0:T(2,128)S(1)}, f32[1,2,6144]{2,1,0:T(2,128)}, u32[]{:S(2)}) copy-start(f32[1,2,6144]{2,1,0:T(2,128)} %param.17) | copy-start | bytes 147460
  13.7 1153.7 %copy-start.2 = (f32[1,2,6144]{2,1,0:T(2,128)S(1)}, f32[1,2,6144]{2,1,0:T(2,128)}, u32[]{:S(2)}) copy-start(f32[1,2,6144]{2,1,0:T(2,128)} %param.18) | copy-start | bytes 147460
  13.7 1153.7 %copy-start.3 = (f32[1,2,6144]{2,1,0:T(2,128)S(1)}, f32[1,2,6144]{2,1,0:T(2,128)}, u32[]{:S(2)}) copy-start(f32[1,2,6144]{2,1,0:T(2,128)} %param.19) | copy-start | bytes 147460
  13.7 1156.2 %copy-start.5 = (f32[1,6144]{1,0:T(1,128)S(1)}, f32[1,6144]{1,0:T(1,128)}, u32[]{:S(2)}) copy-start(f32[1,6144]{1,0:T(1,128)} %param.14) | copy-start | bytes 73732
  13.7 1156.2 %copy-start.6 = (f32[1,6144]{1,0:T(1,128)S(1)}, f32[1,6144]{1,0:T(1,128)}, u32[]{:S(2)}) copy-start(f32[1,6144]{1,0:T(1,128)} %param.15) | copy-start | bytes 73732
  13.7 1156.2 %copy-start.7 = (f32[1,6144]{1,0:T(1,128)S(1)}, f32[1,6144]{1,0:T(1,128)}, u32[]{:S(2)}) copy-start(f32[1,6144]{1,0:T(1,128)} %param.16) | copy-start | bytes 73732
  13.7 1071.4 %all-reduce.7.cloned.1.call-start = ((), (), s32[]{:S(2)}) async-start(), calls=%async_computation.3 | async-start | bytes 6291456
  18.1 1234.9 %all-gather.4.cloned.1.call-start = ((), (), s32[]{:S(2)}) async-start(), calls=%async_computation | async-start | bytes 3194880 | tf_op jit(solution)/shard_map/all_gather | solution.py:54
  1169.9 499.3 %all-gather.6.cloned.1.call-start = ((), (), s32[]{:S(2)}) async-start(), calls=%async_computation.1 | async-start | bytes 6316032 | tf_op jit(solution)/shard_map/all_gather | solution.py:53
Sparse Core Ops, SparseCore 0:
  13.7 274.5 all-reduce.4
  291.7 793.3 all-reduce.6
  1170.0 82.9 all-gather.3
  1255.3 413.8 all-gather.5
where the time goes:
time: 1680 us
  waiting for transfers between devices  1560 us (93%)
  blocking collectives  78.6 us (5%)
    unnamed x6, waiting for transfers between devices  1060 us
    all_gather x1, waiting for transfers between devices, body(): attn_full = lax.all_gather(attn_half, ('expert', 'dp'), axis=0, tiled=True)  412 us
    all_gather x1, waiting for transfers between devices, body(): lax.all_gather(we_new.astype(jnp.bfloat16), 'dp', axis=1, tiled=True)  81.3 us
    psum x1, blocking collectives, body(): summed = lax.psum((sq_attn, sq_exp), ('expert', 'dp'))  78.6 us
  transfers between devices with their start and end apart: 4, of which 4 were waited for; matrix products, arithmetic and copies ran while one was open for 1% of the time, Pallas kernels for 0%

commit v1 on v0

--- a/solution.py
+++ b/solution.py
@@ -50,7 +50,12 @@
     wa_new, ma_new, va_new = adamw(g_attn, w_attn, m_attn, v_attn, factor)
     we_new, me_new, ve_new = adamw(g_exp[None], w_exp, m_exp, v_exp, factor)
     attn_half = wa_new.astype(jnp.bfloat16)
-    attn_full = lax.all_gather(attn_half, ("expert", "dp"), axis=0, tiled=True)
+    attn_full = jnp.concatenate(
+        lax.all_to_all(
+            jnp.stack([attn_half] * lax.axis_size(("expert", "dp"))), ("expert", "dp"), 0, 0
+        ),
+        axis=0,
+    )
     expert_full = lax.all_gather(we_new.astype(jnp.bfloat16), "dp", axis=1, tiled=True)
     return (wa_new, ma_new, va_new, we_new, me_new, ve_new, attn_full, expert_full)
 

time: 1680 us -> 1350 us (0.80)
  waiting for transfers between devices: 1560 us -> 1160 us
  local copies, waits for them, and re-layouts: 13.9 us -> 46.1 us
  other arithmetic: 6.68 us -> 27.3 us
    all_gather x1 -> x0, waiting for transfers between devices: 412 us -> none  [body(): attn_full = lax.all_gather(attn_half, ('expert', 'dp'), axis=0, tiled=True)]
    unnamed x21 -> x23, local copies, waits for them, and re-layouts: 13.2 us -> 40.6 us
    another operation x0 -> x1, other arithmetic: none -> 20.6 us  [body(): jnp.stack([attn_half] * lax.axis_size(('expert', 'dp')))]
    unnamed x6 -> x5, waiting for transfers between devices: 1060 us -> 1060 us
  transfers between devices with their start and end apart: 4 -> 4, of which waited for: 4 -> 3; matrix products, arithmetic and copies ran while one was open for 1% -> 1% of each run, Pallas kernels for 0% -> 0%
where the time goes in v1:
time: 1350 us
  waiting for transfers between devices  1160 us (86%)
  blocking collectives  78.6 us (6%)
  local copies, waits for them, and re-layouts  46.1 us (3%)
  other arithmetic  27.3 us (2%)
  between operations  16.6 us (1%)
    unnamed x5, waiting for transfers between devices  1060 us
    all_gather x1, waiting for transfers between devices, body(): lax.all_gather(we_new.astype(jnp.bfloat16), 'dp', axis=1, tiled=True)  94.8 us
    psum x1, blocking collectives, body(): summed = lax.psum((sq_attn, sq_exp), ('expert', 'dp'))  78.6 us
    unnamed x23, local copies, waits for them, and re-layouts  40.6 us
  transfers between devices with their start and end apart: 4, of which 3 were waited for; matrix products, arithmetic and copies ran while one was open for 1% of the time, Pallas kernels for 0%

profile of v1, /device:TPU:32, one launch (start us, length us, event | category | flops | bytes accessed | tf_op | source)
XLA Modules:
  0.0 1345.2 jit_solution(14662673738310716801)
XLA Ops:
  7.2 0.0 copy-start
  7.2 0.0 all-reduce.5.cloned.1.call-start
  7.2 1.8 copy-done
  9.1 4.6 fusion.9
  13.6 0.0 copy-start.4
  13.6 0.0 all-reduce.5.cloned.1.call-update
  13.7 0.0 copy-start.8
  13.7 0.0 copy-start.5
  13.7 0.0 copy-start.6
  13.7 0.0 copy-start.7
  13.7 0.0 all-reduce.7.cloned.1.call-start
  13.8 0.6 copy-done.4
  14.4 3.7 fusion
  18.1 0.0 all-reduce.7.cloned.1.call-update
  18.1 0.0 copy-done.8
  18.1 0.6 dynamic-slice.1
  19.3 269.0 %all-reduce.5.cloned.1.call-done = f32[256,6144]{1,0:T(8,128)} async-done(((f32[256,6144]{1,0:T(8,128)}), f32[256,6144]{1,0:T(8,128)}) %all-reduce.5.cloned.1.call-update) | async-done | bytes 6291472
  288.4 1.6 multiply_reduce_fusion.1
  289.9 795.2 %all-reduce.7.cloned.1.call-done = f32[128,6144]{1,0:T(8,128)} async-done(((f32[128,6144]{1,0:T(8,128)}), f32[128,6144]{1,0:T(8,128)}) %all-reduce.7.cloned.1.call-update) | async-done | bytes 3145744
  1085.2 1.6 multiply_reduce_fusion
  1088.1 78.6 %psum.16 = f32[]{:T(128)} all-reduce(f32[]{:T(128)S(6)} %add.44), channel_id=1, replica_groups=mesh['expert'=4,'dp'=64] {'expert','dp'}, use_global_device_ids=true, to_apply=%region_2.0 | all-reduce | flops 1 | bytes 8 | tf_op jit(solution)/shard_map/psum | solution.py:46
  1167.4 0.0 copy-done.5
  1167.4 0.0 copy-done.6
  1167.4 0.0 copy-done.7
  1167.5 1.8 convert_reduce_fusion
  1169.2 4.3 stack.2
  1173.5 0.5 broadcast.30
  1174.0 20.6 %reduce.2 = bf16[256,6144]{1,0:T(8,128)(2,1)} reduce(bf16[256,1,6144]{2,1,0:T(2,128)(2,1)} %stack.2, bf16[]{:T(256)} %broadcast.30), dimensions={1}, to_apply=%stack.2.reduce_sub_computation | reduce | bytes 6291458 | tf_op jit(solution)/shard_map/stack | solution.py:55
  1194.6 8.0 reshape.29
  1202.6 0.0 copy-start.1
  1202.6 0.0 copy-start.2
  1202.7 0.0 copy-start.3
  1202.7 8.9 all-to-all-start
  1211.6 0.2 all-gather.2.cloned.1.call-start
  1211.8 0.0 copy-done.1
  1211.8 0.0 copy-done.2
  1211.8 0.0 copy-done.3
  1211.9 1.8 fusion.6
  1213.6 0.7 copy.20
  1214.3 0.0 all-gather.2.cloned.1.call-update
  1214.3 94.8 %all-gather.2.cloned.1.call-done = bf16[1,128,6144]{2,0,1:T(2,128)(2,1)} async-done(((bf16[1,2,6144]{2,0,1:T(2,128)(2,1)}), bf16[1,128,6144]{2,0,1:T(2,128)(2,1)}) %all-gather.2.cloned.1.call-update) | async-done | bytes 1572880 | tf_op jit(solution)/shard_map/all_gather | solution.py:59
  1309.1 3.9 copy.21
  1313.1 0.0 all-to-all-done
  1313.1 19.3 %reshape.30 = bf16[256,1,6144]{2,1,0:T(2,128)(2,1)} reshape(bf16[256,2,3072]{2,1,0:T(2,128)(2,1)} %all-to-all-done) | data formatting | bytes 6291456
  1332.4 6.2 copy.24
Async XLA Ops:
  7.2 1.9 copy-start
  7.2 281.2 %all-reduce.5.cloned.1.call-start = ((), (), s32[]{:S(2)}) async-start(), calls=%async_computation.2 | async-start | bytes 12582912
  13.6 0.8 copy-start.4
  13.7 4.4 copy-start.8
  13.7 1153.8 %copy-start.5 = (f32[1,6144]{1,0:T(1,128)S(1)}, f32[1,6144]{1,0:T(1,128)}, u32[]{:S(2)}) copy-start(f32[1,6144]{1,0:T(1,128)} %param.14) | copy-start | bytes 73732
  13.7 1153.7 %copy-start.6 = (f32[1,6144]{1,0:T(1,128)S(1)}, f32[1,6144]{1,0:T(1,128)}, u32[]{:S(2)}) copy-start(f32[1,6144]{1,0:T(1,128)} %param.15) | copy-start | bytes 73732
  13.7 1153.7 %copy-start.7 = (f32[1,6144]{1,0:T(1,128)S(1)}, f32[1,6144]{1,0:T(1,128)}, u32[]{:S(2)}) copy-start(f32[1,6144]{1,0:T(1,128)} %param.16) | copy-start | bytes 73732
  13.7 1071.5 %all-reduce.7.cloned.1.call-start = ((), (), s32[]{:S(2)}) async-start(), calls=%async_computation.3 | async-start | bytes 6291456
  1202.6 9.2 copy-start.1
  1202.6 9.2 copy-start.2
  1202.7 9.2 copy-start.3
  1202.7 110.4 %all-to-all-start = ((bf16[256,2,3072]{2,1,0:T(2,128)(2,1)}), bf16[256,2,3072]{2,1,0:T(2,128)(2,1)}, u32[]{:S(2)}, u32[]{:S(2)}) async-start(bf16[256,2,3072]{2,1,0:T(2,128)(2,1)} %reshape.29), calls=%async_computation | async-start | bytes 6291456 | tf_op jit(solution)/shard_map/all_to_all | solution.py:54
  1211.6 97.5 %all-gather.2.cloned.1.call-start = ((), (), s32[]{:S(2)}) async-start(), calls=%async_computation.1 | async-start | bytes 3194880 | tf_op jit(solution)/shard_map/all_gather | solution.py:59
Sparse Core Ops, SparseCore 0:
  13.8 274.5 all-reduce.4
  291.7 793.3 all-reduce.6
  1216.5 92.5 all-gather.1
